TPU v7x, 32 devices: a whole 2x2x4 slice. The times are simulated.
32 devices in a mesh: dp: 8 (over y, x, core), seq: 4 (over z).
Axes of the slice: x: 2, y: 2, z: 4, core: 2. Of those that a mesh axis runs over, the one named last changes fastest.
Arguments:
- hidden: bfloat16 [8192, 1792], P(('dp', 'seq')), may hold values from -12.75 to 12.75
- depths: int32 [8192], P(('dp', 'seq')), may hold values from 1 to 3, as said below
- packed_slot_index: int32 [8192], P(('dp', 'seq')), may hold values from -1 to 511, as said below
- value_weight: bfloat16 [1792, 1024], P('dp'), may hold values from -0.125 to 0.125
- output_weight: bfloat16 [1024, 1792], P('dp'), may hold values from -0.1875 to 0.1875
- adapter_down_factor: bfloat16 [1792, 128], P('dp'), may hold values from -0.125 to 0.125
- adapter_up_factor: bfloat16 [1024, 128], P('dp'), may hold values from -0.5 to 0.5
- before_norm_gain: float32 [1792], replicated, may hold values from 0.1 to 1.9
- after_norm_gain: float32 [1792], replicated, may hold values from 0.1 to 1.9
- cotangent: bfloat16 [4096, 1792], P(('dp', 'seq')), may hold values from -6 to 6
Outputs:
- looped: bfloat16 [4096, 1792], P(('dp', 'seq'))
- grad_hidden: bfloat16 [8192, 1792], P(('dp', 'seq'))
- down_factor_gradient: float32 [1792, 128], P('dp', 'seq')
- up_factor_gradient: float32 [1024, 128], P('dp', 'seq')
Inputs may be any that keep to these rules, and one draw needn't show every extreme that they name: `depths`: of the 1024 tokens of one dp index exactly 512 have depth 2 or 3, and all 256 tokens of one seq index are among them. -1 exactly where depths is 1. Over the tokens of one dp index with depth 2 or 3 the slots are a permutation of 0 to 511; packed_slot_index // 128 is the seq index that holds the token's packed row. At most 64 tokens of one device have slots of one seq index, and exactly 64 do in every dp index.
All inputs are finite; a program needn't handle non-finite values.
Results may differ from a plain program's by a relative error of at most 0.01.
Values may be sent and summed in bfloat16 or wider, within the bound.
A program may use at most 64 MiB of HBM per device.

v0:
```python
import math
import jax
import jax.numpy as jnp
from jax import lax
from jax.sharding import PartitionSpec as P

epsilon = 1e-06


def contract_final_axis(left, right):
    return lax.dot_general(
        left, right, (((1,), (1,)), ((), ())), preferred_element_type=jnp.float32
    )


def contract_first(left, right):
    return lax.dot_general(
        left, right, (((0,), (0,)), ((), ())), preferred_element_type=jnp.float32
    )


def layer_forward(
    input_rows,
    cotangent_rows,
    value_weight,
    output_weight,
    adapter_down_factor,
    adapter_up_factor,
    before_norm_gain,
    after_norm_gain,
):
    x_float = input_rows.astype(jnp.float32)
    inv_pre = lax.rsqrt(jnp.mean(x_float * x_float, axis=-1, keepdims=True) + epsilon)
    whitened = x_float * inv_pre
    normalized_rows = (whitened * before_norm_gain).astype(jnp.bfloat16)
    rank_reduced = jnp.dot(
        normalized_rows, adapter_down_factor, preferred_element_type=jnp.float32
    ).astype(jnp.bfloat16)
    projected_rows = (
        jnp.dot(normalized_rows, value_weight, preferred_element_type=jnp.float32)
        + contract_final_axis(rank_reduced, adapter_up_factor)
    ).astype(jnp.bfloat16)
    mixed_out = jnp.dot(projected_rows, output_weight, preferred_element_type=jnp.float32)
    inv_post = lax.rsqrt(jnp.mean(mixed_out * mixed_out, axis=-1, keepdims=True) + epsilon)
    shaped = mixed_out * inv_post
    looped = (x_float + shaped * after_norm_gain).astype(jnp.bfloat16)
    cot_float = cotangent_rows.astype(jnp.float32)
    grad_shaped = cot_float * after_norm_gain
    grad_mixed = (
        inv_post * (grad_shaped - shaped * jnp.mean(grad_shaped * shaped, axis=-1, keepdims=True))
    ).astype(jnp.bfloat16)
    value_gradient = contract_final_axis(grad_mixed, output_weight).astype(jnp.bfloat16)
    low_rank_gradient = jnp.dot(
        value_gradient, adapter_up_factor, preferred_element_type=jnp.float32
    ).astype(jnp.bfloat16)
    normalized_gradient = contract_final_axis(value_gradient, value_weight) + contract_final_axis(
        low_rank_gradient, adapter_down_factor
    )
    grad_white = normalized_gradient * before_norm_gain
    gradient_rows = (
        cot_float
        + inv_pre
        * (grad_white - whitened * jnp.mean(grad_white * whitened, axis=-1, keepdims=True))
    ).astype(jnp.bfloat16)
    down_factor_gradient = contract_first(normalized_rows, low_rank_gradient)
    up_factor_gradient = contract_first(value_gradient, rank_reduced)
    return (looped, gradient_rows, down_factor_gradient, up_factor_gradient)


def body(
    hidden,
    depths,
    packed_slot_index,
    value_weight,
    output_weight,
    adapter_down_factor,
    adapter_up_factor,
    before_norm_gain,
    after_norm_gain,
    cotangent,
):
    seq_count = lax.axis_size("seq")
    own_index = lax.axis_index("seq")
    tok_count = hidden.shape[0]
    act_rows = cotangent.shape[0]
    value_full, out_full, down_full, up_full = (
        lax.all_gather(value_weight, "dp", axis=0, tiled=True),
        lax.all_gather(output_weight, "dp", axis=0, tiled=True),
        lax.all_gather(adapter_down_factor, "dp", axis=0, tiled=True),
        lax.all_gather(adapter_up_factor, "dp", axis=0, tiled=True),
    )
    depth_all, slot_all = (
        lax.all_gather(depths, "seq", axis=0, tiled=True),
        lax.all_gather(packed_slot_index, "seq", axis=0, tiled=True),
    )
    active_all = depth_all >= 2
    dest_all = jnp.where(active_all, slot_all // act_rows, -1)
    pos_all = jnp.where(active_all, slot_all % act_rows, 0)
    mine = active_all & (dest_all == own_index)
    active = depths >= 2
    zero_row = jnp.zeros((), jnp.bfloat16)
    rows_all = lax.all_gather(hidden, "seq", axis=0, tiled=True)
    source = (
        jnp.zeros((act_rows,), jnp.int32)
        .at[jnp.where(mine, pos_all, act_rows)]
        .set(jnp.arange(seq_count * tok_count, dtype=jnp.int32), mode="drop")
    )
    packed = jnp.take(rows_all, source, axis=0)
    looped, gradient_rows, down_factor_gradient, up_factor_gradient = layer_forward(
        packed,
        cotangent,
        value_full,
        out_full,
        down_full,
        up_full,
        before_norm_gain,
        after_norm_gain,
    )
    grads_all = lax.all_gather(gradient_rows, "seq", axis=0, tiled=True)
    picked = jnp.take(grads_all, jnp.maximum(packed_slot_index, 0), axis=0)
    grad_hidden = jnp.where(active[:, None], picked, zero_row)
    grad_scale = 1.0 / math.sqrt(seq_count * act_rows * lax.axis_size("dp"))
    down_term = down_factor_gradient * grad_scale
    up_term = up_factor_gradient * grad_scale
    down_mid, up_mid = (
        lax.psum_scatter(
            down_term.astype(jnp.bfloat16), "seq", scatter_dimension=1, tiled=True
        ).astype(jnp.float32),
        lax.psum_scatter(
            up_term.astype(jnp.bfloat16), "seq", scatter_dimension=1, tiled=True
        ).astype(jnp.float32),
    )
    down_sum, up_sum = (
        lax.psum_scatter(down_mid, "dp", scatter_dimension=0, tiled=True),
        lax.psum_scatter(up_mid, "dp", scatter_dimension=0, tiled=True),
    )
    return (looped, grad_hidden, down_sum, up_sum)


def solution(mesh):
    placed = (
        P(("dp", "seq"), None),
        P(("dp", "seq")),
        P(("dp", "seq")),
        P("dp", None),
        P("dp", None),
        P("dp", None),
        P("dp", None),
        P(),
        P(),
        P(("dp", "seq"), None),
    )
    return jax.shard_map(
        body,
        mesh=mesh,
        in_specs=placed,
        out_specs=(P(("dp", "seq"), None), P(("dp", "seq"), None), P("dp", "seq"), P("dp", "seq")),
        check_vma=False,
    )
```

profile of v0, /device:TPU:0, one launch (start us, length us, event | category | flops | bytes accessed | tf_op | source)
XLA Modules:
  0.0 329.3 jit_solution(13722843027043391828)
XLA Ops:
  7.2 0.0 all-gather.7.cloned.1.call-start
  7.2 0.7 all-gather.7.cloned.1.call-update
  7.9 0.0 all-gather.9.cloned.1.call-start
  8.0 0.7 all-gather.9.cloned.1.call-update
  8.7 0.0 all-gather.11.cloned.1.call-start
  8.7 0.7 all-gather.11.cloned.1.call-update
  9.4 0.0 reduce-scatter.7.cloned.1.call-start
  9.4 12.8 %all-gather = s32[4,1,256]{2,1,0:T(1,128)S(1)} all-gather(s32[1,1,256]{2,1,0:T(1,128)} %bitcast.21), channel_id=1, replica_groups=mesh['dp'=8,'seq'=4] {'seq'}, dimensions={0}, use_global_device_ids=true | all-gather | bytes 5120 | tf_op jit(solution)/shard_map/all_gather | solution.py:93
  22.3 8.1 %all-gather.1 = s32[4,1,256]{2,1,0:T(1,128)S(1)} all-gather(s32[1,1,256]{2,1,0:T(1,128)} %bitcast.20), channel_id=1, replica_groups=mesh['dp'=8,'seq'=4] {'seq'}, dimensions={0}, use_global_device_ids=true | all-gather | bytes 5120 | tf_op jit(solution)/shard_map/all_gather | solution.py:94
  30.4 4.3 %scatter_custom_fusion = s32[128]{0:T(128)S(1)} fusion(s32[1024]{0:T(1024)S(1)} %compare_select_fusion, s32[1024]{0:T(1024)S(1)} %iota.3, s32[]{:T(128)} %constant.69.clone.1), kind=kCustom, calls=%fused_computation.69 | custom fusion | bytes 516 | tf_op jit(solution)/shard_map/scatter | solution.py:106
  34.8 9.5 %all_gather.29 = bf16[1024,128]{1,0:T(8,128)(2,1)S(1)} all-gather(bf16[128,128]{1,0:T(8,128)(2,1)} %param.16), channel_id=1, replica_groups=mesh['dp'=8,'seq'=4] {'dp'}, dimensions={0}, use_global_device_ids=true | all-gather | bytes 294912 | tf_op jit(solution)/shard_map/all_gather | solution.py:90
  44.3 9.5 %all_gather.28 = bf16[1792,128]{1,0:T(8,128)(2,1)S(1)} all-gather(bf16[224,128]{1,0:T(8,128)(2,1)} %param.15), channel_id=1, replica_groups=mesh['dp'=8,'seq'=4] {'dp'}, dimensions={0}, use_global_device_ids=true | all-gather | bytes 516096 | tf_op jit(solution)/shard_map/all_gather | solution.py:89
  53.8 30.7 %all-gather.7.cloned.1.call-done = bf16[1024,1792]{1,0:T(8,128)(2,1)} async-done(((bf16[256,1792]{1,0:T(8,128)(2,1)}), bf16[1024,1792]{1,0:T(8,128)(2,1)}) %all-gather.7.cloned.1.call-update) | async-done | bytes 3670032 | tf_op jit(solution)/shard_map/all_gather | solution.py:102
  84.5 3.8 %gather_fusion = bf16[128,1792]{1,0:T(8,128)(2,1)S(1)} fusion(bf16[1024,1792]{1,0:T(8,128)(2,1)} %all-gather.7.cloned.1.call-done, s32[1024]{0:T(1024)S(1)} %pad_clamp_fusion.1), kind=kCustom, calls=%fused_computation | custom fusion | bytes 918016 | tf_op jit(solution)/shard_map/jit(_take)/gather | solution.py:108
  88.4 0.3 fusion.18
  88.7 0.4 convolution_convert_fusion.1
  89.0 30.5 %all-gather.9.cloned.1.call-done = bf16[1792,1024]{1,0:T(8,128)(2,1)} async-done(((bf16[224,1024]{1,0:T(8,128)(2,1)}), bf16[1792,1024]{1,0:T(8,128)(2,1)}) %all-gather.9.cloned.1.call-update) | async-done | bytes 3670032 | tf_op jit(solution)/shard_map/all_gather | solution.py:87
  119.5 2.7 fusion.37
  122.3 0.0 copy-start
  122.3 33.7 %all-gather.11.cloned.1.call-done = bf16[1024,1792]{1,0:T(8,128)(2,1)} async-done(((bf16[128,1792]{1,0:T(8,128)(2,1)}), bf16[1024,1792]{1,0:T(8,128)(2,1)}) %all-gather.11.cloned.1.call-update) | async-done | bytes 3670032 | tf_op jit(solution)/shard_map/all_gather | solution.py:88
  156.0 2.9 multiply_reduce_fusion
  158.9 1.1 fusion.10
  160.0 3.4 %convolution_convert_fusion = bf16[128,1024]{1,0:T(8,128)(2,1)S(1)} fusion(bf16[1024,1792]{1,0:T(8,128)(2,1)} %all-gather.11.cloned.1.call-done, bf16[128,1792]{1,0:T(8,128)(2,1)S(1)} %copy-done, f32[128,1792]{1,0:T(8,128)S(1)} %get-tuple-element.7, f32[128]{0:T(128)S(1)} %broadcast_multiply_fusion.1, f32[1792]{0:T(1024)S(1)} %copy-done.1, ...), kind=kOutput, calls=%fused_computation.15 | convolution fusion | flops 471498752 | bytes 5316608 | tf_op jit(solution)/shard_map/dot_general | solution.py:11
  163.4 0.2 convolution_convert_fusion.2
  163.6 1.2 fusion.1
  164.8 0.0 reduce-scatter.7.cloned.1.call-update
  164.8 0.0 reduce-scatter.9.cloned.1.call-start
  164.9 1.0 fusion.6
  165.8 0.0 reduce-scatter.9.cloned.1.call-update
  165.8 0.0 reduce-scatter.13.cloned.1.call-start
  165.9 3.4 %fusion.39 = f32[128,1792]{1,0:T(8,128)S(1)} fusion(bf16[128,1024]{1,0:T(8,128)(2,1)S(1)} %convolution_convert_fusion, bf16[1792,1024]{1,0:T(8,128)(2,1)} %all-gather.9.cloned.1.call-done), kind=kOutput, calls=%fused_computation.72 | convolution fusion | flops 469762048 | bytes 4849664 | tf_op jit(solution)/shard_map/dot_general | solution.py:11
  169.3 0.4 fusion.15
  169.8 16.2 %reduce-scatter.7.cloned.1.call-done = bf16[1792,32]{0,1:T(8,128)(2,1)} async-done(((bf16[1792,128]{0,1:T(8,128)(2,1)}), bf16[1792,32]{0,1:T(8,128)(2,1)}) %reduce-scatter.7.cloned.1.call-update) | async-done | bytes 114704 | tf_op jit(solution)/shard_map/reduce_scatter | solution.py:126
  186.0 2.0 copy.14
  188.0 0.0 reduce-scatter.13.cloned.1.call-update
  188.0 0.0 all-gather.13.cloned.1.call-start
  188.1 1.3 fusion.13
  189.4 0.0 all-gather.13.cloned.1.call-update
  189.4 0.0 reduce-scatter.11.cloned.1.call-start
  189.6 16.7 %reduce-scatter.9.cloned.1.call-done = bf16[1024,32]{0,1:T(8,128)(2,1)} async-done(((bf16[1024,128]{0,1:T(8,128)(2,1)}), bf16[1024,32]{0,1:T(8,128)(2,1)}) %reduce-scatter.9.cloned.1.call-update) | async-done | bytes 65552 | tf_op jit(solution)/shard_map/reduce_scatter | solution.py:129
  206.3 1.5 convert_element_type.55
  207.8 0.0 reduce-scatter.11.cloned.1.call-update
  207.8 35.8 %reduce-scatter.13.cloned.1.call-done = f32[224,32]{1,0:T(8,128)} async-done(((f32[1792,32]{1,0:T(8,128)}), f32[224,32]{1,0:T(8,128)}) %reduce-scatter.13.cloned.1.call-update) | async-done | bytes 28688
  243.6 1.6 copy.15
  245.2 41.4 %all-gather.13.cloned.1.call-done = bf16[512,1792]{1,0:T(8,128)(2,1)} async-done(((bf16[128,1792]{1,0:T(8,128)(2,1)}), bf16[512,1792]{1,0:T(8,128)(2,1)}) %all-gather.13.cloned.1.call-update) | async-done | bytes 1835024 | tf_op jit(solution)/shard_map/all_gather | solution.py:119
  286.6 3.9 %gather_fusion.1 = bf16[256,1792]{1,0:T(8,128)(2,1)S(1)} fusion(bf16[512,1792]{1,0:T(8,128)(2,1)} %all-gather.13.cloned.1.call-done, s32[1024]{0:T(1024)S(1)} %pad_clamp_fusion), kind=kCustom, calls=%fused_computation.1 | custom fusion | bytes 1836032 | tf_op jit(solution)/shard_map/jit(_take)/gather | solution.py:120
  290.5 1.1 select_select_fusion
  291.6 30.8 %reduce-scatter.11.cloned.1.call-done = f32[128,32]{0,1:T(8,128)} async-done(((f32[1024,32]{0,1:T(8,128)}), f32[128,32]{0,1:T(8,128)}) %reduce-scatter.11.cloned.1.call-update) | async-done | bytes 16400 | tf_op jit(solution)/shard_map/reduce_scatter | solution.py:135
  (24 shorter events, 0.1 us)
Async XLA Ops:
  7.2 81.5 %copy-start.2 = (f32[1792]{0:T(1024)S(1)}, f32[1792]{0:T(1024)}, u32[]{:S(2)}) copy-start(f32[1792]{0:T(1024)} %param.17) | copy-start | bytes 21508
  7.2 77.3 %all-gather.7.cloned.1.call-start = ((), (), s32[]{:S(2)}) async-start(), calls=%async_computation.4 | async-start | bytes 4587520 | tf_op jit(solution)/shard_map/all_gather | solution.py:102
  7.9 111.6 %all-gather.9.cloned.1.call-start = ((), (), s32[]{:S(2)}) async-start(), calls=%async_computation.5 | async-start | bytes 4128768 | tf_op jit(solution)/shard_map/all_gather | solution.py:87
  8.7 147.3 %all-gather.11.cloned.1.call-start = ((), (), s32[]{:S(2)}) async-start(), calls=%async_computation.6 | async-start | bytes 4128768 | tf_op jit(solution)/shard_map/all_gather | solution.py:88
  9.4 176.6 %reduce-scatter.7.cloned.1.call-start = ((), (), s32[]{:S(2)}) async-start(), calls=%async_computation.8 | async-start | bytes 573440 | tf_op jit(solution)/shard_map/reduce_scatter | solution.py:126
  122.3 36.7 %copy-start = (bf16[128,1792]{1,0:T(8,128)(2,1)S(1)}, bf16[128,1792]{1,0:T(8,128)(2,1)}, u32[]{:S(2)}) copy-start(bf16[128,1792]{1,0:T(8,128)(2,1)} %param.19) | copy-start | bytes 1376260
  122.3 36.6 %copy-start.1 = (f32[1792]{0:T(1024)S(1)}, f32[1792]{0:T(1024)}, u32[]{:S(2)}) copy-start(f32[1792]{0:T(1024)} %param.18) | copy-start | bytes 21508
  164.8 41.5 %reduce-scatter.9.cloned.1.call-start = ((), (), s32[]{:S(2)}) async-start(), calls=%async_computation.9 | async-start | bytes 327680 | tf_op jit(solution)/shard_map/reduce_scatter | solution.py:129
  165.8 77.8 %reduce-scatter.13.cloned.1.call-start = ((), (), s32[]{:S(2)}) async-start(), calls=%async_computation.11 | async-start | bytes 1032192
  169.3 20.2 %copy-start.3 = (s32[256]{0:T(256)S(1)}, s32[256]{0:T(256)}, u32[]{:S(2)}) copy-start(s32[256]{0:T(256)} %param.12) | copy-start | bytes 3076
  169.3 20.3 %copy-start.4 = (s32[256]{0:T(256)S(1)}, s32[256]{0:T(256)}, u32[]{:S(2)}) copy-start(s32[256]{0:T(256)} %param.11) | copy-start | bytes 3076
  188.0 98.6 %all-gather.13.cloned.1.call-start = ((), (), s32[]{:S(2)}) async-start(), calls=%async_computation.7 | async-start | bytes 2293760 | tf_op jit(solution)/shard_map/all_gather | solution.py:119
  189.4 133.0 %reduce-scatter.11.cloned.1.call-start = ((), (), s32[]{:S(2)}) async-start(), calls=%async_computation.10 | async-start | bytes 147456 | tf_op jit(solution)/shard_map/reduce_scatter | solution.py:135
Sparse Core Ops, SparseCore 0:
  9.6 74.8 all-gather.6
  86.4 33.0 all-gather.8
  121.4 34.5 all-gather.10
  164.9 20.9 reduce-scatter.6
  188.2 18.0 reduce-scatter.8
  209.9 33.6 reduce-scatter.12
  245.2 41.3 all-gather.12
  290.2 32.2 reduce-scatter.10
where the time goes:
time: 330 us; the launch traced here: 329 us
  waiting for transfers between devices  238 us (72%)
  blocking collectives  39.9 us (12%)
  local copies, waits for them, and re-layouts  15.7 us (5%)
  matrix products  15.5 us (5%)
  between operations  14.3 us (4%)
  other arithmetic  5.43 us (2%)
    all_gather x1, waiting for transfers between devices, body(): grads_all = lax.all_gather(gradient_rows, 'seq', axis=0, tiled=True)  41.4 us
    unnamed x9, waiting for transfers between devices  38 us
    all_gather x1, waiting for transfers between devices, body(): lax.all_gather(output_weight, 'dp', axis=0, tiled=True)  33.7 us
    reduce_scatter x1, waiting for transfers between devices, body(): lax.psum_scatter(up_mid, 'dp', scatter_dimension=0, tiled=True)  30.8 us
    all_gather x1, waiting for transfers between devices, body(): rows_all = lax.all_gather(hidden, 'seq', axis=0, tiled=True)  30.7 us
    all_gather x1, waiting for transfers between devices, body(): lax.all_gather(value_weight, 'dp', axis=0, tiled=True)  30.5 us
    reduce_scatter x1, waiting for transfers between devices, body(): lax.psum_scatter(up_term.astype(jnp.bfloat16), 'seq', scatter_dimension=1...  16.7 us
    reduce_scatter x1, waiting for transfers between devices, body(): lax.psum_scatter(down_term.astype(jnp.bfloat16), 'seq', scatter_dimension...  16.2 us
  transfers between devices with their start and end apart: 8, of which 8 were waited for; matrix products, arithmetic and copies ran while one was open for 8% of the time, Pallas kernels for 0%

commit v1 on v0

--- a/solution.py
+++ b/solution.py
@@ -90,7 +90,9 @@
         lax.all_gather(adapter_up_factor, "dp", axis=0, tiled=True),
     )
     depth_all, slot_all = (
-        lax.all_gather(depths, "seq", axis=0, tiled=True),
+        jnp.concatenate(
+            lax.all_to_all(jnp.stack([depths] * lax.axis_size("seq")), "seq", 0, 0), axis=0
+        ),
         lax.all_gather(packed_slot_index, "seq", axis=0, tiled=True),
     )
     active_all = depth_all >= 2

time: 330 us -> 330 us (level)
  blocking collectives: 39.9 us -> 30.8 us
  starting transfers between devices: 0.32 us -> 6.6 us
    all_gather x1 -> x0, blocking collectives: 12.8 us -> none  [body(): lax.all_gather(depths, 'seq', axis=0, tiled=True)]
    all_to_all x0 -> x1, starting transfers between devices: none -> 6.32 us  [body(): lax.all_to_all(jnp.stack([depths] * lax.axis_size('seq')), 'seq', 0, 0)]
    all_gather x1, blocking collectives: 8.08 us -> 11.8 us  [body(): lax.all_gather(packed_slot_index, 'seq', axis=0, tiled=True)]
  transfers between devices with their start and end apart: 8 -> 9, of which waited for: 8 -> 8; matrix products, arithmetic and copies ran while one was open for 8% -> 9% of each run, Pallas kernels for 0% -> 0%
where the time goes in v1:
time: 330 us; the launch traced here: 329 us
  waiting for transfers between devices  240 us (73%)
  blocking collectives  30.8 us (9%)
  local copies, waits for them, and re-layouts  17 us (5%)
  matrix products  15.5 us (5%)
  between operations  14.3 us (4%)
  starting transfers between devices  6.6 us (2%)
  other arithmetic  5.44 us (2%)
    all_gather x1, waiting for transfers between devices, body(): grads_all = lax.all_gather(gradient_rows, 'seq', axis=0, tiled=True)  41.4 us
    unnamed x9, waiting for transfers between devices  38 us
    all_gather x1, waiting for transfers between devices, body(): lax.all_gather(output_weight, 'dp', axis=0, tiled=True)  33.7 us
    all_gather x1, waiting for transfers between devices, body(): rows_all = lax.all_gather(hidden, 'seq', axis=0, tiled=True)  32.3 us
    reduce_scatter x1, waiting for transfers between devices, body(): lax.psum_scatter(up_mid, 'dp', scatter_dimension=0, tiled=True)  30.8 us
    all_gather x1, waiting for transfers between devices, body(): lax.all_gather(value_weight, 'dp', axis=0, tiled=True)  30.6 us
    reduce_scatter x1, waiting for transfers between devices, body(): lax.psum_scatter(up_term.astype(jnp.bfloat16), 'seq', scatter_dimension=1...  16.7 us
    reduce_scatter x1, waiting for transfers between devices, body(): lax.psum_scatter(down_term.astype(jnp.bfloat16), 'seq', scatter_dimension...  16.2 us
  transfers between devices with their start and end apart: 9, of which 8 were waited for; matrix products, arithmetic and copies ran while one was open for 9% of the time, Pallas kernels for 0%

profile of v1, /device:TPU:0, one launch (start us, length us, event | category | flops | bytes accessed | tf_op | source)
XLA Modules:
  0.0 329.4 jit_solution(14723840790087526818)
XLA Ops:
  7.2 0.0 all-gather.6.cloned.1.call-start
  7.2 0.7 all-gather.6.cloned.1.call-update
  7.9 0.0 all-gather.8.cloned.1.call-start
  8.0 0.7 all-gather.8.cloned.1.call-update
  8.7 0.0 all-gather.10.cloned.1.call-start
  8.7 0.7 all-gather.10.cloned.1.call-update
  9.4 1.3 stack.2
  10.7 6.3 %all-to-all-start = ((s32[4,1,256]{2,1,0:T(1,128)}), s32[4,1,256]{2,1,0:T(1,128)S(1)}, u32[]{:S(2)}, u32[]{:S(2)}) async-start(s32[4,1,256]{2,1,0:T(1,128)} %stack.2), calls=%async_computation | async-start | bytes 8192 | tf_op jit(solution)/shard_map/all_to_all | solution.py:94
  17.0 10.0 %all_gather.24 = bf16[1792,128]{1,0:T(8,128)(2,1)S(1)} all-gather(bf16[224,128]{1,0:T(8,128)(2,1)} %param.15), channel_id=1, replica_groups=mesh['dp'=8,'seq'=4] {'dp'}, dimensions={0}, use_global_device_ids=true | all-gather | bytes 516096 | tf_op jit(solution)/shard_map/all_gather | solution.py:89
  27.0 9.0 %all_gather.25 = bf16[1024,128]{1,0:T(8,128)(2,1)S(1)} all-gather(bf16[128,128]{1,0:T(8,128)(2,1)} %param.16), channel_id=1, replica_groups=mesh['dp'=8,'seq'=4] {'dp'}, dimensions={0}, use_global_device_ids=true | all-gather | bytes 294912 | tf_op jit(solution)/shard_map/all_gather | solution.py:90
  36.0 11.8 %all-gather = s32[4,1,256]{2,1,0:T(1,128)S(1)} all-gather(s32[1,1,256]{2,1,0:T(1,128)} %bitcast.19), channel_id=1, replica_groups=mesh['dp'=8,'seq'=4] {'seq'}, dimensions={0}, use_global_device_ids=true | all-gather | bytes 5120 | tf_op jit(solution)/shard_map/all_gather | solution.py:96
  47.8 4.3 %scatter_custom_fusion = s32[128]{0:T(128)S(1)} fusion(s32[1024]{0:T(1024)S(1)} %compare_select_fusion, s32[1024]{0:T(1024)S(1)} %iota.3, s32[]{:T(128)} %constant.69.clone.1), kind=kCustom, calls=%fused_computation.69 | custom fusion | bytes 516 | tf_op jit(solution)/shard_map/scatter | solution.py:108
  52.2 32.3 %all-gather.6.cloned.1.call-done = bf16[1024,1792]{1,0:T(8,128)(2,1)} async-done(((bf16[256,1792]{1,0:T(8,128)(2,1)}), bf16[1024,1792]{1,0:T(8,128)(2,1)}) %all-gather.6.cloned.1.call-update) | async-done | bytes 3670032 | tf_op jit(solution)/shard_map/all_gather | solution.py:104
  84.5 3.8 %gather_fusion = bf16[128,1792]{1,0:T(8,128)(2,1)S(1)} fusion(bf16[1024,1792]{1,0:T(8,128)(2,1)} %all-gather.6.cloned.1.call-done, s32[1024]{0:T(1024)S(1)} %pad_clamp_fusion.1), kind=kCustom, calls=%fused_computation | custom fusion | bytes 918016 | tf_op jit(solution)/shard_map/jit(_take)/gather | solution.py:110
  88.3 0.3 fusion.18
  88.6 0.4 convolution_convert_fusion.1
  89.0 30.6 %all-gather.8.cloned.1.call-done = bf16[1792,1024]{1,0:T(8,128)(2,1)} async-done(((bf16[224,1024]{1,0:T(8,128)(2,1)}), bf16[1792,1024]{1,0:T(8,128)(2,1)}) %all-gather.8.cloned.1.call-update) | async-done | bytes 3670032 | tf_op jit(solution)/shard_map/all_gather | solution.py:87
  119.5 2.7 fusion.37
  122.3 0.0 copy-start.1
  122.3 33.7 %all-gather.10.cloned.1.call-done = bf16[1024,1792]{1,0:T(8,128)(2,1)} async-done(((bf16[128,1792]{1,0:T(8,128)(2,1)}), bf16[1024,1792]{1,0:T(8,128)(2,1)}) %all-gather.10.cloned.1.call-update) | async-done | bytes 3670032 | tf_op jit(solution)/shard_map/all_gather | solution.py:88
  156.0 2.9 multiply_reduce_fusion
  158.9 1.1 fusion.10
  160.0 3.4 %convolution_convert_fusion = bf16[128,1024]{1,0:T(8,128)(2,1)S(1)} fusion(bf16[1024,1792]{1,0:T(8,128)(2,1)} %all-gather.10.cloned.1.call-done, bf16[128,1792]{1,0:T(8,128)(2,1)S(1)} %copy-done, f32[128,1792]{1,0:T(8,128)S(1)} %get-tuple-element.7, f32[128]{0:T(128)S(1)} %broadcast_multiply_fusion.1, f32[1792]{0:T(1024)S(1)} %copy-done.1, ...), kind=kOutput, calls=%fused_computation.15 | convolution fusion | flops 471498752 | bytes 5316608 | tf_op jit(solution)/shard_map/dot_general | solution.py:11
  163.4 0.2 convolution_convert_fusion.2
  163.6 1.2 fusion.1
  164.8 0.0 reduce-scatter.7.cloned.1.call-update
  164.8 0.0 reduce-scatter.9.cloned.1.call-start
  164.9 1.0 fusion.6
  165.8 0.0 reduce-scatter.9.cloned.1.call-update
  165.9 0.0 reduce-scatter.13.cloned.1.call-start
  165.9 3.4 %fusion.39 = f32[128,1792]{1,0:T(8,128)S(1)} fusion(bf16[128,1024]{1,0:T(8,128)(2,1)S(1)} %convolution_convert_fusion, bf16[1792,1024]{1,0:T(8,128)(2,1)} %all-gather.8.cloned.1.call-done), kind=kOutput, calls=%fused_computation.72 | convolution fusion | flops 469762048 | bytes 4849664 | tf_op jit(solution)/shard_map/dot_general | solution.py:11
  169.3 0.4 fusion.15
  169.8 16.2 %reduce-scatter.7.cloned.1.call-done = bf16[1792,32]{0,1:T(8,128)(2,1)} async-done(((bf16[1792,128]{0,1:T(8,128)(2,1)}), bf16[1792,32]{0,1:T(8,128)(2,1)}) %reduce-scatter.7.cloned.1.call-update) | async-done | bytes 114704 | tf_op jit(solution)/shard_map/reduce_scatter | solution.py:128
  186.0 2.0 copy.14
  188.0 0.0 reduce-scatter.13.cloned.1.call-update
  188.1 0.0 all-gather.12.cloned.1.call-start
  188.1 1.4 fusion.13
  189.5 0.0 all-gather.12.cloned.1.call-update
  189.5 0.0 reduce-scatter.11.cloned.1.call-start
  189.6 16.7 %reduce-scatter.9.cloned.1.call-done = bf16[1024,32]{0,1:T(8,128)(2,1)} async-done(((bf16[1024,128]{0,1:T(8,128)(2,1)}), bf16[1024,32]{0,1:T(8,128)(2,1)}) %reduce-scatter.9.cloned.1.call-update) | async-done | bytes 65552 | tf_op jit(solution)/shard_map/reduce_scatter | solution.py:131
  206.3 1.5 convert_element_type.55
  207.8 0.0 reduce-scatter.11.cloned.1.call-update
  207.8 35.9 %reduce-scatter.13.cloned.1.call-done = f32[224,32]{1,0:T(8,128)} async-done(((f32[1792,32]{1,0:T(8,128)}), f32[224,32]{1,0:T(8,128)}) %reduce-scatter.13.cloned.1.call-update) | async-done | bytes 28688
  243.7 1.6 copy.15
  245.3 41.4 %all-gather.12.cloned.1.call-done = bf16[512,1792]{1,0:T(8,128)(2,1)} async-done(((bf16[128,1792]{1,0:T(8,128)(2,1)}), bf16[512,1792]{1,0:T(8,128)(2,1)}) %all-gather.12.cloned.1.call-update) | async-done | bytes 1835024 | tf_op jit(solution)/shard_map/all_gather | solution.py:121
  286.7 3.9 %gather_fusion.1 = bf16[256,1792]{1,0:T(8,128)(2,1)S(1)} fusion(bf16[512,1792]{1,0:T(8,128)(2,1)} %all-gather.12.cloned.1.call-done, s32[1024]{0:T(1024)S(1)} %pad_clamp_fusion), kind=kCustom, calls=%fused_computation.1 | custom fusion | bytes 1836032 | tf_op jit(solution)/shard_map/jit(_take)/gather | solution.py:122
  290.6 1.1 select_select_fusion
  291.7 30.8 %reduce-scatter.11.cloned.1.call-done = f32[128,32]{0,1:T(8,128)} async-done(((f32[1024,32]{0,1:T(8,128)}), f32[128,32]{0,1:T(8,128)}) %reduce-scatter.11.cloned.1.call-update) | async-done | bytes 16400 | tf_op jit(solution)/shard_map/reduce_scatter | solution.py:137
  (26 shorter events, 0.2 us)
Async XLA Ops:
  7.2 81.4 %copy-start.2 = (f32[1792]{0:T(1024)S(1)}, f32[1792]{0:T(1024)}, u32[]{:S(2)}) copy-start(f32[1792]{0:T(1024)} %param.17) | copy-start | bytes 21508
  7.2 77.3 %all-gather.6.cloned.1.call-start = ((), (), s32[]{:S(2)}) async-start(), calls=%async_computation.5 | async-start | bytes 4587520 | tf_op jit(solution)/shard_map/all_gather | solution.py:104
  7.9 111.6 %all-gather.8.cloned.1.call-start = ((), (), s32[]{:S(2)}) async-start(), calls=%async_computation.6 | async-start | bytes 4128768 | tf_op jit(solution)/shard_map/all_gather | solution.py:87
  8.7 147.3 %all-gather.10.cloned.1.call-start = ((), (), s32[]{:S(2)}) async-start(), calls=%async_computation.7 | async-start | bytes 4128768 | tf_op jit(solution)/shard_map/all_gather | solution.py:88
  10.7 37.1 %all-to-all-start = ((s32[4,1,256]{2,1,0:T(1,128)}), s32[4,1,256]{2,1,0:T(1,128)S(1)}, u32[]{:S(2)}, u32[]{:S(2)}) async-start(s32[4,1,256]{2,1,0:T(1,128)} %stack.2), calls=%async_computation | async-start | bytes 8192 | tf_op jit(solution)/shard_map/all_to_all | solution.py:94
  17.0 169.0 %reduce-scatter.7.cloned.1.call-start = ((), (), s32[]{:S(2)}) async-start(), calls=%async_computation.9 | async-start | bytes 573440 | tf_op jit(solution)/shard_map/reduce_scatter | solution.py:128
  122.3 36.6 %copy-start = (bf16[128,1792]{1,0:T(8,128)(2,1)S(1)}, bf16[128,1792]{1,0:T(8,128)(2,1)}, u32[]{:S(2)}) copy-start(bf16[128,1792]{1,0:T(8,128)(2,1)} %param.19) | copy-start | bytes 1376260
  122.3 36.6 %copy-start.1 = (f32[1792]{0:T(1024)S(1)}, f32[1792]{0:T(1024)}, u32[]{:S(2)}) copy-start(f32[1792]{0:T(1024)} %param.18) | copy-start | bytes 21508
  164.8 41.5 %reduce-scatter.9.cloned.1.call-start = ((), (), s32[]{:S(2)}) async-start(), calls=%async_computation.10 | async-start | bytes 327680 | tf_op jit(solution)/shard_map/reduce_scatter | solution.py:131
  165.9 77.8 %reduce-scatter.13.cloned.1.call-start = ((), (), s32[]{:S(2)}) async-start(), calls=%async_computation.12 | async-start | bytes 1032192
  169.3 20.3 %copy-start.3 = (s32[256]{0:T(256)S(1)}, s32[256]{0:T(256)}, u32[]{:S(2)}) copy-start(s32[256]{0:T(256)} %param.12) | copy-start | bytes 3076
  169.3 20.3 %copy-start.4 = (s32[256]{0:T(256)S(1)}, s32[256]{0:T(256)}, u32[]{:S(2)}) copy-start(s32[256]{0:T(256)} %param.11) | copy-start | bytes 3076
  188.1 98.6 %all-gather.12.cloned.1.call-start = ((), (), s32[]{:S(2)}) async-start(), calls=%async_computation.8 | async-start | bytes 2293760 | tf_op jit(solution)/shard_map/all_gather | solution.py:121
  189.5 133.0 %reduce-scatter.11.cloned.1.call-start = ((), (), s32[]{:S(2)}) async-start(), calls=%async_computation.11 | async-start | bytes 147456 | tf_op jit(solution)/shard_map/reduce_scatter | solution.py:137
Sparse Core Ops, SparseCore 0:
  9.6 74.8 all-gather.5
  86.3 33.1 all-gather.7
  121.4 34.5 all-gather.9
  164.9 21.0 reduce-scatter.6
  188.2 18.0 reduce-scatter.8
  209.9 33.7 reduce-scatter.12
  245.3 41.3 all-gather.11
  290.2 32.2 reduce-scatter.10
